TPU v7x, 256 devices: a whole 4x4x8 slice. The times are simulated.
256 devices in a mesh: blk: 32 (over z, x_lo, core), head: 8 (over x_hi, y).
Axes of the slice: x: 4 (x_hi: 2, x_lo: 2; x = x_hi * 2 + x_lo), y: 4, z: 8, core: 2. Of those that a mesh axis runs over, the one named last changes fastest.
Arguments:
- query_tokens: bfloat16 [16384, 3072], P(('blk', 'head')), may hold values from -12 to 12
- key_tokens: bfloat16 [16384, 3072], P(('blk', 'head')), may hold values from -6 to 6
- value_tokens: bfloat16 [16384, 3072], P(('blk', 'head')), may hold values from -6 to 6
- out_weight: bfloat16 [3072, 3072], P('head'), may hold values from -1.75 to 1.75
- kv_blocks: int32 [128, 16], P('blk'), may hold values from -1 to 127, as said below
Outputs:
- projected: bfloat16 [16384, 3072], P(('blk', 'head'))
Inputs may be any that keep to these rules, and one draw needn't show every extreme that they name: `kv_blocks`: row i lists the key blocks of 128 tokens that query block i attends to; let G = floor(i / 4). Entry 0 is i. Entry 1 is one of the blocks 4 * M to 4 * M + 3 with M = (G + 16) mod 32. Entry j >= 2 is -1 (absent) or one of the blocks 4 * (G + o) to 4 * (G + o) + 3, with o = j // 2 for even j and o = -(j - 1) // 2 for odd j; it is present whenever j < 8 and those blocks exist. Entries of one row are distinct.
All inputs are finite; a program needn't handle non-finite values.
Results may differ from a plain program's by a relative error of at most 0.012.
Values may be sent and summed in bfloat16 or wider, within the bound.
A program may use at most 128 MiB of HBM per device.

v0:
```python
import math
import jax
import jax.numpy as jnp
from jax import lax
from jax.sharding import PartitionSpec as P

HD = 128
masked_low = -1e30


def sparse_attend(query_sets, key_sets, value_sets, present):
    blocks_dev = present.shape[0]
    slots = present.shape[1]
    block_rows = query_sets.shape[2]
    scaling = 1.0 / math.sqrt(HD)
    allowed = jnp.broadcast_to(present[:, :, None], (blocks_dev, slots, block_rows)).reshape(
        blocks_dev, slots * block_rows
    )
    scores = (
        jnp.einsum("hbqd,hbkd->hbqk", query_sets, key_sets, preferred_element_type=jnp.float32)
        * scaling
    )
    mask_full = allowed[None, :, None, :]
    peak_value = jnp.max(jnp.where(mask_full, scores, masked_low), axis=-1, keepdims=True)
    weights = jnp.where(mask_full, jnp.exp(scores - peak_value), 0.0)
    denom = jnp.sum(weights, axis=-1)
    outputs = jnp.einsum(
        "hbqk,hbkd->hbqd",
        weights.astype(jnp.bfloat16),
        value_sets,
        preferred_element_type=jnp.float32,
    )
    return outputs / denom[..., None]


def on_device(query_tokens, key_tokens, value_tokens, out_weight, kv_blocks):
    queries, key_rows, value_rows = (
        lax.all_to_all(query_tokens, "head", split_axis=1, concat_axis=0, tiled=True),
        lax.all_to_all(key_tokens, "head", split_axis=1, concat_axis=0, tiled=True),
        lax.all_to_all(value_tokens, "head", split_axis=1, concat_axis=0, tiled=True),
    )
    row_total = queries.shape[0]
    feature_width = queries.shape[1]
    heads_dev = feature_width // HD
    blocks_dev = kv_blocks.shape[0]
    block_rows = row_total // blocks_dev
    slots = kv_blocks.shape[1]
    query_heads = queries.reshape(row_total, heads_dev, HD).transpose(1, 0, 2)
    query_sets = query_heads.reshape(heads_dev, blocks_dev, block_rows, HD)
    key_heads = key_rows.reshape(row_total, heads_dev, HD).transpose(1, 0, 2)
    value_heads = value_rows.reshape(row_total, heads_dev, HD).transpose(1, 0, 2)
    present = kv_blocks >= 0
    safe_index = jnp.maximum(kv_blocks, 0)
    gathered_keys, gathered_values = (
        lax.all_gather(key_heads, "blk", axis=1, tiled=True),
        lax.all_gather(value_heads, "blk", axis=1, tiled=True),
    )
    total_blocks = gathered_keys.shape[1] // block_rows
    source_keys = gathered_keys.reshape(heads_dev, total_blocks, block_rows, HD)
    source_values = gathered_values.reshape(heads_dev, total_blocks, block_rows, HD)
    flat_index = safe_index.reshape(blocks_dev * slots)
    key_sets = jnp.take(source_keys, flat_index, axis=1).reshape(
        heads_dev, blocks_dev, slots * block_rows, HD
    )
    value_sets = jnp.take(source_values, flat_index, axis=1).reshape(
        heads_dev, blocks_dev, slots * block_rows, HD
    )
    outputs = sparse_attend(query_sets, key_sets, value_sets, present)
    attended = (
        outputs.reshape(heads_dev, row_total, HD)
        .transpose(1, 0, 2)
        .reshape(row_total, feature_width)
    )
    attended = attended.astype(jnp.bfloat16)
    return lax.psum_scatter(
        jnp.dot(attended, out_weight, preferred_element_type=jnp.float32).astype(jnp.bfloat16),
        "head",
        scatter_dimension=0,
        tiled=True,
    )


def solution(mesh):
    placed = (
        P(("blk", "head"), None),
        P(("blk", "head"), None),
        P(("blk", "head"), None),
        P("head", None),
        P("blk", None),
    )
    return jax.shard_map(
        on_device, mesh=mesh, in_specs=placed, out_specs=P(("blk", "head"), None), check_vma=False
    )
```

profile of v0, /device:TPU:32, one launch (start us, length us, event | category | flops | bytes accessed | tf_op | source)
XLA Modules:
  0.0 322.1 jit_solution(16858350131159604797)
XLA Ops:
  6.5 0.0 copy-start
  6.5 0.0 copy-start.1
  6.5 0.0 all-gather.3.cloned.1.call-start
  6.5 1.2 copy.46
  7.7 16.9 %all_to_all.48 = bf16[64,8,384]{2,0,1:T(8,128)(2,1)S(1)} all-to-all(bf16[64,8,384]{2,0,1:T(8,128)(2,1)S(1)} %bitcast.64), channel_id=1, replica_groups=mesh['blk'=32,'head'=8] {'head'}, dimensions={1} | all-to-all | bytes 786432 | tf_op jit(solution)/shard_map/all_to_all | solution.py:39
  24.7 0.1 reshape.52
  24.8 0.8 copy.26
  25.6 0.0 all-gather.3.cloned.1.call-update
  25.6 0.0 all-gather.5.cloned.1.call-start
  25.6 1.0 copy.44
  26.7 12.0 %all_to_all.49 = bf16[64,8,384]{2,0,1:T(8,128)(2,1)S(1)} all-to-all(bf16[64,8,384]{2,0,1:T(8,128)(2,1)S(1)} %bitcast.65), channel_id=1, replica_groups=mesh['blk'=32,'head'=8] {'head'}, dimensions={1} | all-to-all | bytes 786432 | tf_op jit(solution)/shard_map/all_to_all | solution.py:40
  38.7 0.1 reshape.58
  38.8 0.8 copy.31
  39.7 0.0 all-gather.5.cloned.1.call-update
  39.7 1.9 copy.45
  41.5 3.5 %all-to-all-start.1 = ((bf16[64,8,384]{2,0,1:T(8,128)(2,1)}), bf16[64,8,384]{2,0,1:T(8,128)(2,1)S(1)}, u32[]{:S(2)}, u32[]{:S(2)}) async-start(bf16[64,8,384]{2,0,1:T(8,128)(2,1)} %bitcast.51), calls=%async_computation.1 | async-start | bytes 786432 | tf_op jit(solution)/shard_map/all_to_all | solution.py:38
  45.0 0.0 reduce-scatter.2.cloned.1.call-start
  45.1 0.0 copy-done.1
  45.1 0.1 reshape.54
  45.2 0.1 broadcast_bitcast_fusion
  45.3 8.9 %all-to-all-done.1 = bf16[64,8,384]{2,0,1:T(8,128)(2,1)S(1)} async-done(((bf16[64,8,384]{2,0,1:T(8,128)(2,1)}), bf16[64,8,384]{2,0,1:T(8,128)(2,1)S(1)}, u32[]{:S(2)}, u32[]{:S(2)}) %all-to-all-start.1) | async-done | bytes 393248 | tf_op jit(solution)/shard_map/all_to_all | solution.py:38
  54.2 0.1 reshape.56
  54.3 0.1 copy.29
  54.4 51.7 %all-gather.3.cloned.1.call-done = bf16[3,16384,128]{2,1,0:T(8,128)(2,1)} async-done(((bf16[3,512,128]{2,1,0:T(8,128)(2,1)}), bf16[3,16384,128]{2,1,0:T(8,128)(2,1)}) %all-gather.3.cloned.1.call-update) | async-done | bytes 12582928 | tf_op jit(solution)/shard_map/all_gather | solution.py:55
  106.1 8.6 %gather_fusion = bf16[64,3,128,128]{3,2,1,0:T(8,128)(2,1)} fusion(bf16[3,128,128,128]{3,2,1,0:T(8,128)(2,1)} %bitcast.56, s32[1024]{0:T(1024)S(1)} %pad_clamp_fusion), kind=kCustom, calls=%fused_computation.clone | custom fusion | bytes 12583168 | tf_op jit(solution)/shard_map/jit(_take)/gather | solution.py:62
  114.7 72.9 %all-gather.5.cloned.1.call-done = bf16[3,16384,128]{2,1,0:T(8,128)(2,1)} async-done(((bf16[3,512,128]{2,1,0:T(8,128)(2,1)}), bf16[3,16384,128]{2,1,0:T(8,128)(2,1)}) %all-gather.5.cloned.1.call-update) | async-done | bytes 12582928 | tf_op jit(solution)/shard_map/all_gather | solution.py:56
  187.6 8.5 %gather_fusion.1 = bf16[64,3,128,128]{3,2,1,0:T(8,128)(2,1)} fusion(bf16[3,128,128,128]{3,2,1,0:T(8,128)(2,1)} %bitcast.57, s32[1024]{0:T(1024)S(1)} %pad_clamp_fusion), kind=kCustom, calls=%fused_computation.1.clone | custom fusion | bytes 12583168 | tf_op jit(solution)/shard_map/jit(_take)/gather | solution.py:65
  196.1 5.5 %select_bitcast_fusion.1 = (bf16[3,64,128,128]{3,2,0,1:T(8,128)(2,1)S(1)}, bf16[3,64,128,128]{3,2,0,1:T(8,128)(2,1)S(1)}) fusion(bf16[64,3,128,128]{3,2,1,0:T(8,128)(2,1)} %gather_fusion, pred[64]{0:T(512)(128)(4,1)S(1)} %compare_and_fusion, bf16[64,3,128,128]{3,2,1,0:T(8,128)(2,1)} %gather_fusion.1), kind=kLoop, calls=%fused_computation.11 | loop fusion | flops 6291456 | bytes 25165888 | tf_op jit(solution)/shard_map/jit(_take)/select_n | solution.py:62
  201.7 4.0 %copy.27 = bf16[3,64,128,128]{3,2,1,0:T(8,128)(2,1)} copy(bf16[3,64,128,128]{3,2,0,1:T(8,128)(2,1)S(1)} %get-tuple-element.6) | data formatting | bytes 12582912 | tf_op jit(solution)/shard_map/jit(_take)/select_n | solution.py:62
  205.7 4.0 %copy.32 = bf16[3,64,128,128]{3,2,1,0:T(8,128)(2,1)} copy(bf16[3,64,128,128]{3,2,0,1:T(8,128)(2,1)S(1)} %get-tuple-element.7) | data formatting | bytes 12582912 | tf_op jit(solution)/shard_map/jit(_take)/select_n | solution.py:65
  209.7 10.3 %bitcast_reduce_fusion = (f32[3,4,128]{2,1,0:T(4,128)S(1)}, bf16[3,4,2048,128]{3,2,1,0:T(8,128)(2,1)}) fusion(pred[4,2048]{1,0:T(4,128)(4,1)S(1)} %bitcast.72, bf16[3,4,2048,128]{3,2,1,0:T(8,128)(2,1)} %bitcast.54, bf16[3,4,128,128]{3,2,1,0:T(8,128)(2,1)S(1)} %bitcast.66), kind=kOutput, calls=%fused_computation.3 | convolution fusion | flops 1632634880 | bytes 12990464 | tf_op jit(solution)/shard_map/sub | solution.py:25
  220.0 6.6 %fusion.10 = bf16[3,4,128,128]{3,2,1,0:T(8,128)(2,1)S(1)} fusion(bf16[3,4,2048,128]{3,2,1,0:T(8,128)(2,1)} %bitcast.55, f32[3,4,128]{2,1,0:T(4,128)S(1)} %get-tuple-element.8, bf16[3,4,2048,128]{3,2,1,0:T(8,128)(2,1)} %get-tuple-element.9), kind=kOutput, calls=%fused_computation.17 | convolution fusion | flops 805699584 | bytes 12982272 | tf_op jit(solution)/shard_map/hbqk,hbkd->hbqd/dot_general | solution.py:27
  226.7 0.2 copy.34
  226.9 0.0 copy-done
  226.9 3.5 %convolution_convert_fusion = bf16[512,3072]{1,0:T(8,128)(2,1)} fusion(bf16[512,384]{0,1:T(8,128)(2,1)S(1)} %bitcast.71, bf16[384,3072]{1,0:T(8,128)(2,1)S(1)} %copy-done), kind=kOutput, calls=%fused_computation.15 | convolution fusion | flops 1209532416 | bytes 5898240 | tf_op jit(solution)/shard_map/dot_general | solution.py:76
  230.3 0.0 reduce-scatter.2.cloned.1.call-update
  230.4 85.2 %reduce-scatter.2.cloned.1.call-done = bf16[64,3072]{1,0:T(8,128)(2,1)} async-done(((bf16[512,3072]{1,0:T(8,128)(2,1)}), bf16[64,3072]{1,0:T(8,128)(2,1)}) %reduce-scatter.2.cloned.1.call-update) | async-done | bytes 393232 | tf_op jit(solution)/shard_map/reduce_scatter | solution.py:75
  (6 shorter events, 0.0 us)
Async XLA Ops:
  6.5 220.3 %copy-start = (bf16[384,3072]{1,0:T(8,128)(2,1)S(1)}, bf16[384,3072]{1,0:T(8,128)(2,1)}, u32[]{:S(2)}) copy-start(bf16[384,3072]{1,0:T(8,128)(2,1)} %param.10) | copy-start | bytes 7077892
  6.5 38.5 %copy-start.1 = (s32[4,16]{1,0:T(4,128)S(1)}, s32[4,16]{1,0:T(4,128)}, u32[]{:S(2)}) copy-start(s32[4,16]{1,0:T(4,128)} %param.11) | copy-start | bytes 772
  6.5 99.5 %all-gather.3.cloned.1.call-start = ((), (), s32[]{:S(2)}) async-start(), calls=%async_computation.4 | async-start | bytes 12976128 | tf_op jit(solution)/shard_map/all_gather | solution.py:55
  25.6 162.0 %all-gather.5.cloned.1.call-start = ((), (), s32[]{:S(2)}) async-start(), calls=%async_computation.5 | async-start | bytes 12976128 | tf_op jit(solution)/shard_map/all_gather | solution.py:56
  41.5 12.6 %all-to-all-start.1 = ((bf16[64,8,384]{2,0,1:T(8,128)(2,1)}), bf16[64,8,384]{2,0,1:T(8,128)(2,1)S(1)}, u32[]{:S(2)}, u32[]{:S(2)}) async-start(bf16[64,8,384]{2,0,1:T(8,128)(2,1)} %bitcast.51), calls=%async_computation.1 | async-start | bytes 786432 | tf_op jit(solution)/shard_map/all_to_all | solution.py:38
  45.0 270.6 %reduce-scatter.2.cloned.1.call-start = ((), (), s32[]{:S(2)}) async-start(), calls=%async_computation.6 | async-start | bytes 3538944 | tf_op jit(solution)/shard_map/reduce_scatter | solution.py:75
Sparse Core Ops, SparseCore 0:
  25.7 80.2 all-gather.2
  107.9 79.6 all-gather.4
  230.5 85.0 reduce-scatter.1
where the time goes:
time: 323 us; the launch traced here: 322 us
  waiting for transfers between devices  219 us (68%)
  local copies, waits for them, and re-layouts  31.7 us (10%)
  blocking collectives  28.9 us (9%)
  matrix products  20.4 us (6%)
  between operations  13.2 us (4%)
  other arithmetic  5.58 us (2%)
  starting transfers between devices  3.54 us (1%)
    reduce_scatter x1, waiting for transfers between devices, on_device(): lax.psum_scatter(jnp.dot(attended, out_weight, preferred_element_type=jnp...  85.2 us
    all_gather x1, waiting for transfers between devices, on_device(): lax.all_gather(value_heads, 'blk', axis=1, tiled=True)  72.9 us
    all_gather x1, waiting for transfers between devices, on_device(): lax.all_gather(key_heads, 'blk', axis=1, tiled=True)  51.7 us
    all_to_all x1, blocking collectives, on_device(): lax.all_to_all(key_tokens, 'head', split_axis=1, concat_axis=0, tiled=True)  16.9 us
    all_to_all x1, blocking collectives, on_device(): lax.all_to_all(value_tokens, 'head', split_axis=1, concat_axis=0, tiled=T...  12 us
    sub x1, matrix products, sparse_attend(): weights = jnp.where(mask_full, jnp.exp(scores - peak_value), 0.0)  10.3 us
    all_to_all x1, waiting for transfers between devices, on_device(): lax.all_to_all(query_tokens, 'head', split_axis=1, concat_axis=0, tiled=T...  8.89 us
    gather x1, local copies, waits for them, and re-layouts, on_device(): jnp.take(source_keys, flat_index, axis=1)  8.63 us
  transfers between devices with their start and end apart: 4, of which 4 were waited for; matrix products, arithmetic and copies ran while one was open for 4% of the time, Pallas kernels for 0%

commit v1 on v0

--- a/solution.py
+++ b/solution.py
@@ -1,3 +1,4 @@
+import functools
 import math
 import jax
 import jax.numpy as jnp
@@ -6,6 +7,21 @@
 
 HD = 128
 masked_low = -1e30
+
+
+def bring_space(frame, a_name):
+    return jnp.concatenate(
+        lax.all_to_all(
+            jnp.stack(jnp.split(frame, lax.axis_size(a_name), 1), axis=0),
+            axis_name=a_name,
+            split_axis=0,
+            concat_axis=0,
+        ),
+        axis=0,
+    )
+
+
+fit_the_roots = functools.partial(bring_space, a_name="head")
 
 
 def sparse_attend(query_sets, key_sets, value_sets, present):
@@ -35,7 +51,7 @@
 
 def on_device(query_tokens, key_tokens, value_tokens, out_weight, kv_blocks):
     queries, key_rows, value_rows = (
-        lax.all_to_all(query_tokens, "head", split_axis=1, concat_axis=0, tiled=True),
+        fit_the_roots(query_tokens),
         lax.all_to_all(key_tokens, "head", split_axis=1, concat_axis=0, tiled=True),
         lax.all_to_all(value_tokens, "head", split_axis=1, concat_axis=0, tiled=True),
     )

time: 323 us -> 322 us (level)
  waiting for transfers between devices: 219 us -> 209 us
  local copies, waits for them, and re-layouts: 31.7 us -> 41.1 us
    unnamed x6 -> x13, local copies, waits for them, and re-layouts: 0.1 us -> 10 us
    all_gather x1, waiting for transfers between devices: 51.7 us -> 42.7 us  [on_device(): lax.all_gather(key_heads, 'blk', axis=1, tiled=True)]
  transfers between devices with their start and end apart: 4 -> 4, of which waited for: 4 -> 4; matrix products, arithmetic and copies ran while one was open for 4% -> 7% of each run, Pallas kernels for 0% -> 0%
where the time goes in v1:
time: 322 us; the launch traced here: 321 us
  waiting for transfers between devices  209 us (65%)
  local copies, waits for them, and re-layouts  41.1 us (13%)
  blocking collectives  28.9 us (9%)
  matrix products  19.8 us (6%)
  between operations  13.2 us (4%)
  other arithmetic  5.58 us (2%)
  starting transfers between devices  3.54 us (1%)
    reduce_scatter x1, waiting for transfers between devices, on_device(): lax.psum_scatter(jnp.dot(attended, out_weight, preferred_element_type=jnp...  85.2 us
    all_gather x1, waiting for transfers between devices, on_device(): lax.all_gather(value_heads, 'blk', axis=1, tiled=True)  72.3 us
    all_gather x1, waiting for transfers between devices, on_device(): lax.all_gather(key_heads, 'blk', axis=1, tiled=True)  42.7 us
    all_to_all x1, blocking collectives, on_device(): lax.all_to_all(key_tokens, 'head', split_axis=1, concat_axis=0, tiled=True)  16.9 us
    all_to_all x1, blocking collectives, on_device(): lax.all_to_all(value_tokens, 'head', split_axis=1, concat_axis=0, tiled=T...  12 us
    unnamed x13, local copies, waits for them, and re-layouts  10 us
    sub x1, matrix products, sparse_attend(): weights = jnp.where(mask_full, jnp.exp(scores - peak_value), 0.0)  9.97 us
    all_to_all x1, waiting for transfers between devices, bring_space(): lax.all_to_all(jnp.stack(jnp.split(frame, lax.axis_size(a_name), 1), axis...  8.89 us
  transfers between devices with their start and end apart: 4, of which 4 were waited for; matrix products, arithmetic and copies ran while one was open for 7% of the time, Pallas kernels for 0%

profile of v1, /device:TPU:32, one launch (start us, length us, event | category | flops | bytes accessed | tf_op | source)
XLA Modules:
  0.0 321.5 jit_solution(5286598714474629961)
XLA Ops:
  6.5 0.0 copy-start
  6.5 0.0 copy-start.1
  6.5 0.0 all-gather.3.cloned.1.call-start
  6.5 1.2 copy.36
  7.7 16.9 %all_to_all.37 = bf16[64,8,384]{2,0,1:T(8,128)(2,1)S(1)} all-to-all(bf16[64,8,384]{2,0,1:T(8,128)(2,1)S(1)} %bitcast.64), channel_id=1, replica_groups=mesh['blk'=32,'head'=8] {'head'}, dimensions={1} | all-to-all | bytes 786432 | tf_op jit(solution)/shard_map/all_to_all | solution.py:55
  24.7 0.1 reshape.46
  24.8 0.8 copy.23
  25.6 0.0 all-gather.3.cloned.1.call-update
  25.6 0.0 all-gather.5.cloned.1.call-start
  25.6 1.0 copy.35
  26.7 12.0 %all_to_all.38 = bf16[64,8,384]{2,0,1:T(8,128)(2,1)S(1)} all-to-all(bf16[64,8,384]{2,0,1:T(8,128)(2,1)S(1)} %bitcast.65), channel_id=1, replica_groups=mesh['blk'=32,'head'=8] {'head'}, dimensions={1} | all-to-all | bytes 786432 | tf_op jit(solution)/shard_map/all_to_all | solution.py:56
  38.7 0.1 reshape.50
  38.8 0.8 copy.26
  39.7 0.0 all-gather.5.cloned.1.call-update
  39.7 1.4 bitcast_dynamic-update-slice_fusion.7
  41.1 1.4 bitcast_dynamic-update-slice_fusion.6
  42.5 1.4 bitcast_dynamic-update-slice_fusion.5
  43.9 1.4 bitcast_dynamic-update-slice_fusion.4
  45.4 1.4 bitcast_dynamic-update-slice_fusion.3
  46.8 1.4 bitcast_dynamic-update-slice_fusion.2
  48.2 1.4 bitcast_dynamic-update-slice_fusion.1
  49.6 1.4 bitcast_dynamic-update-slice_fusion
  51.0 3.5 %all-to-all-start = ((bf16[8,64,384]{2,1,0:T(8,128)(2,1)}), bf16[8,64,384]{2,1,0:T(8,128)(2,1)S(1)}, u32[]{:S(2)}, u32[]{:S(2)}) async-start(bf16[8,64,384]{2,1,0:T(8,128)(2,1)} %bitcast_dynamic-update-slice_fusion), calls=%async_computation | async-start | bytes 786432 | tf_op jit(solution)/shard_map/all_to_all | solution.py:14
  54.5 0.0 reduce-scatter.2.cloned.1.call-start
  54.5 0.0 copy-done.1
  54.6 0.1 reshape.48
  54.7 0.1 broadcast_bitcast_fusion
  54.8 8.9 %all-to-all-done = bf16[8,64,384]{2,1,0:T(8,128)(2,1)S(1)} async-done(((bf16[8,64,384]{2,1,0:T(8,128)(2,1)}), bf16[8,64,384]{2,1,0:T(8,128)(2,1)S(1)}, u32[]{:S(2)}, u32[]{:S(2)}) %all-to-all-start) | async-done | bytes 393248 | tf_op jit(solution)/shard_map/all_to_all | solution.py:14
  63.7 0.1 reshape_reshape.3
  63.8 0.1 copy.21
  63.9 42.7 %all-gather.3.cloned.1.call-done = bf16[3,16384,128]{2,1,0:T(8,128)(2,1)} async-done(((bf16[3,512,128]{2,1,0:T(8,128)(2,1)}), bf16[3,16384,128]{2,1,0:T(8,128)(2,1)}) %all-gather.3.cloned.1.call-update) | async-done | bytes 12582928 | tf_op jit(solution)/shard_map/all_gather | solution.py:71
  106.6 8.6 %gather_fusion = bf16[64,3,128,128]{3,2,1,0:T(8,128)(2,1)} fusion(bf16[3,128,128,128]{3,2,1,0:T(8,128)(2,1)} %bitcast.57, s32[1024]{0:T(1024)S(1)} %pad_clamp_fusion), kind=kCustom, calls=%fused_computation.clone | custom fusion | bytes 12583168 | tf_op jit(solution)/shard_map/jit(_take)/gather | solution.py:78
  115.2 72.3 %all-gather.5.cloned.1.call-done = bf16[3,16384,128]{2,1,0:T(8,128)(2,1)} async-done(((bf16[3,512,128]{2,1,0:T(8,128)(2,1)}), bf16[3,16384,128]{2,1,0:T(8,128)(2,1)}) %all-gather.5.cloned.1.call-update) | async-done | bytes 12582928 | tf_op jit(solution)/shard_map/all_gather | solution.py:72
  187.5 8.5 %gather_fusion.1 = bf16[64,3,128,128]{3,2,1,0:T(8,128)(2,1)} fusion(bf16[3,128,128,128]{3,2,1,0:T(8,128)(2,1)} %bitcast.58, s32[1024]{0:T(1024)S(1)} %pad_clamp_fusion), kind=kCustom, calls=%fused_computation.1.clone | custom fusion | bytes 12583168 | tf_op jit(solution)/shard_map/jit(_take)/gather | solution.py:81
  196.1 5.5 %select_bitcast_fusion.1 = (bf16[3,64,128,128]{3,2,0,1:T(8,128)(2,1)S(1)}, bf16[3,64,128,128]{3,2,0,1:T(8,128)(2,1)S(1)}) fusion(bf16[64,3,128,128]{3,2,1,0:T(8,128)(2,1)} %gather_fusion, pred[64]{0:T(512)(128)(4,1)S(1)} %compare_and_fusion, bf16[64,3,128,128]{3,2,1,0:T(8,128)(2,1)} %gather_fusion.1), kind=kLoop, calls=%fused_computation.8 | loop fusion | flops 6291456 | bytes 25165888 | tf_op jit(solution)/shard_map/jit(_take)/select_n | solution.py:78
  201.6 4.0 %copy.24 = bf16[3,64,128,128]{3,2,1,0:T(8,128)(2,1)} copy(bf16[3,64,128,128]{3,2,0,1:T(8,128)(2,1)S(1)} %get-tuple-element.6) | data formatting | bytes 12582912 | tf_op jit(solution)/shard_map/jit(_take)/select_n | solution.py:78
  205.6 4.0 %copy.27 = bf16[3,64,128,128]{3,2,1,0:T(8,128)(2,1)} copy(bf16[3,64,128,128]{3,2,0,1:T(8,128)(2,1)S(1)} %get-tuple-element.7) | data formatting | bytes 12582912 | tf_op jit(solution)/shard_map/jit(_take)/select_n | solution.py:81
  209.7 10.0 %fusion.20 = (f32[3,4,128]{2,1,0:T(4,128)S(1)}, bf16[3,4,128,2048]{3,2,1,0:T(8,128)(2,1)}) fusion(pred[4,2048]{1,0:T(4,128)(4,1)S(1)} %bitcast.71, bf16[3,4,128,128]{3,2,1,0:T(8,128)(2,1)S(1)} %bitcast.66, bf16[3,4,2048,128]{3,2,1,0:T(8,128)(2,1)} %bitcast.55), kind=kOutput, calls=%fused_computation.37 | convolution fusion | flops 1632634880 | bytes 12990464 | tf_op jit(solution)/shard_map/sub | solution.py:41
  219.6 6.4 %fusion.13 = bf16[3,4,128,128]{3,2,1,0:T(8,128)(2,1)S(1)} fusion(bf16[3,4,2048,128]{3,2,1,0:T(8,128)(2,1)} %bitcast.56, bf16[3,4,128,2048]{3,2,1,0:T(8,128)(2,1)} %get-tuple-element.9, f32[3,4,128]{2,1,0:T(4,128)S(1)} %get-tuple-element.8), kind=kOutput, calls=%fused_computation.16 | convolution fusion | flops 805699584 | bytes 12982272 | tf_op jit(solution)/shard_map/hbqk,hbkd->hbqd/dot_general | solution.py:43
  226.0 0.2 copy.28
  226.2 0.0 copy-done
  226.2 3.5 %convolution_convert_fusion = bf16[512,3072]{1,0:T(8,128)(2,1)} fusion(bf16[512,384]{0,1:T(8,128)(2,1)S(1)} %bitcast.70, bf16[384,3072]{1,0:T(8,128)(2,1)S(1)} %copy-done), kind=kOutput, calls=%fused_computation.14 | convolution fusion | flops 1209532416 | bytes 5898240 | tf_op jit(solution)/shard_map/dot_general | solution.py:92
  229.7 0.0 reduce-scatter.2.cloned.1.call-update
  229.7 85.2 %reduce-scatter.2.cloned.1.call-done = bf16[64,3072]{1,0:T(8,128)(2,1)} async-done(((bf16[512,3072]{1,0:T(8,128)(2,1)}), bf16[64,3072]{1,0:T(8,128)(2,1)}) %reduce-scatter.2.cloned.1.call-update) | async-done | bytes 393232 | tf_op jit(solution)/shard_map/reduce_scatter | solution.py:91
  (6 shorter events, 0.0 us)
Async XLA Ops:
  6.5 219.7 %copy-start = (bf16[384,3072]{1,0:T(8,128)(2,1)S(1)}, bf16[384,3072]{1,0:T(8,128)(2,1)}, u32[]{:S(2)}) copy-start(bf16[384,3072]{1,0:T(8,128)(2,1)} %param.10) | copy-start | bytes 7077892
  6.5 48.0 %copy-start.1 = (s32[4,16]{1,0:T(4,128)S(1)}, s32[4,16]{1,0:T(4,128)}, u32[]{:S(2)}) copy-start(s32[4,16]{1,0:T(4,128)} %param.11) | copy-start | bytes 772
  6.5 100.1 %all-gather.3.cloned.1.call-start = ((), (), s32[]{:S(2)}) async-start(), calls=%async_computation.4 | async-start | bytes 12976128 | tf_op jit(solution)/shard_map/all_gather | solution.py:71
  25.6 161.9 %all-gather.5.cloned.1.call-start = ((), (), s32[]{:S(2)}) async-start(), calls=%async_computation.5 | async-start | bytes 12976128 | tf_op jit(solution)/shard_map/all_gather | solution.py:72
  51.0 12.6 %all-to-all-start = ((bf16[8,64,384]{2,1,0:T(8,128)(2,1)}), bf16[8,64,384]{2,1,0:T(8,128)(2,1)S(1)}, u32[]{:S(2)}, u32[]{:S(2)}) async-start(bf16[8,64,384]{2,1,0:T(8,128)(2,1)} %bitcast_dynamic-update-slice_fusion), calls=%async_computation | async-start | bytes 786432 | tf_op jit(solution)/shard_map/all_to_all | solution.py:14
  54.5 260.5 %reduce-scatter.2.cloned.1.call-start = ((), (), s32[]{:S(2)}) async-start(), calls=%async_computation.6 | async-start | bytes 3538944 | tf_op jit(solution)/shard_map/reduce_scatter | solution.py:91
Sparse Core Ops, SparseCore 0:
  25.7 80.8 all-gather.2
  108.5 79.0 all-gather.4
  229.8 85.0 reduce-scatter.1
